TPU v7x, 32 devices: a whole 2x2x4 slice. The times are simulated.
32 devices in a mesh: dp: 4 (over y, core), seq: 8 (over z, x).
Axes of the slice: x: 2, y: 2, z: 4, core: 2. Of those that a mesh axis runs over, the one named last changes fastest.
Arguments:
- tokens: bfloat16 [4, 24, 256, 1280], P('dp', 'seq'), may hold values from -6 to 6
- clip_ids: int32 [4, 24], P('dp'), may hold values from 0 to 5, never falling along the last dimension, each value on 1 to 12 neighbouring positions
- ln_gain: float32 [1280], replicated, may hold values from 0.1 to 1.9
- w_qkv: bfloat16 [1280, 1920], P(None, 'dp'), may hold values from -0.15625 to 0.15625
- w_out: bfloat16 [640, 1280], P(None, 'dp'), may hold values from -0.25 to 0.25
Outputs:
- output: bfloat16 [4, 24, 256, 1280], P('dp', 'seq')
Inputs may be any that keep to these rules, and one draw needn't show every extreme that they name: `clip_ids`: in each batch the clip numbers never fall along the frames, every clip number occurs, each clip covers 1 to 12 consecutive frames, and some clip covers exactly 12.
All inputs are finite; a program needn't handle non-finite values.
Results may differ from a plain program's by a relative error of at most 0.006.
Values may be sent and summed in bfloat16 or wider, within the bound.
A program may use at most 64 MiB of HBM per device.

v0:
```python
import math
import jax
import jax.numpy as jnp
from jax import lax
from jax.sharding import PartitionSpec as P

HS = 80
HEADS = 8
HD = 640
norm_eps = 1e-05


def layer_norm(block, ln_gain):
    values = block.astype(jnp.float32)
    center = jnp.mean(values, axis=-1, keepdims=True)
    spread = jnp.mean(jnp.square(values - center), axis=-1, keepdims=True)
    return ((values - center) * lax.rsqrt(spread + norm_eps) * ln_gain).astype(jnp.bfloat16)


def split_heads(projected):
    queries = (projected[:, :HD] * (1.0 / math.sqrt(HS))).astype(jnp.bfloat16)
    keys = projected[:, HD : 2 * HD].astype(jnp.bfloat16)
    values = projected[:, 2 * HD :].astype(jnp.bfloat16)
    return (queries, keys, values)


def attend(queries, keys, values, clip_row):
    scores = jnp.einsum("flhe,glhe->lhfg", queries, keys, preferred_element_type=jnp.float32)
    same_clip = clip_row[:, None] == clip_row[None, :]
    raised = jnp.where(same_clip, jnp.exp(scores), jnp.zeros_like(scores))
    attn_probs = (raised / jnp.sum(raised, axis=-1, keepdims=True)).astype(jnp.bfloat16)
    return jnp.einsum(
        "lhfg,glhe->flhe", attn_probs, values, preferred_element_type=jnp.float32
    ).astype(jnp.bfloat16)


def shards(tokens, clip_ids, ln_gain, w_qkv, w_out):
    width = tokens.shape[3]
    clip_row = clip_ids[0]
    frames = clip_row.shape[0]
    local_frames = tokens.shape[1]
    patches = tokens.shape[2]
    moved = lax.all_to_all(tokens, "seq", split_axis=2, concat_axis=1, tiled=True)
    places = moved.shape[2]
    normed = layer_norm(moved, ln_gain).reshape(frames * places, width)

    def column_block(piece, start):
        return jnp.dot(normed, piece, preferred_element_type=jnp.float32)

    queries, keys, values = split_heads(
        column_block(lax.all_gather(w_qkv, "dp", axis=1, tiled=True), jnp.int32(0))
    )
    head_shape = (frames, places, HEADS, HS)
    mixed = attend(
        queries.reshape(head_shape), keys.reshape(head_shape), values.reshape(head_shape), clip_row
    )
    mixed = lax.all_to_all(
        mixed.reshape(1, frames, places, HD), "seq", split_axis=1, concat_axis=2, tiled=True
    )
    row_count = local_frames * patches
    rows_in = mixed.reshape(row_count, HD)

    def column_block(piece, start):
        return jnp.dot(rows_in, piece, preferred_element_type=jnp.float32)

    update = column_block(lax.all_gather(w_out, "dp", axis=1, tiled=True), jnp.int32(0))
    summed = tokens.reshape(row_count, width).astype(jnp.float32) + update
    return summed.astype(jnp.bfloat16).reshape(tokens.shape)


def solution(mesh):
    placed = (P("dp", "seq", None, None), P("dp", None), P(), P(None, "dp"), P(None, "dp"))
    return jax.shard_map(
        shards, mesh=mesh, in_specs=placed, out_specs=P("dp", "seq", None, None), check_vma=False
    )
```

profile of v0, /device:TPU:0, one launch (start us, length us, event | category | flops | bytes accessed | tf_op | source)
XLA Modules:
  0.0 151.9 jit_solution(18149255715372341711)
XLA Ops:
  6.5 0.0 all-gather.3.cloned.1.call-start
  6.5 0.7 all-gather.3.cloned.1.call-update
  7.3 4.8 %copy.35 = bf16[1,3,256,1280]{3,1,0,2:T(4,128)(2,1)} copy(bf16[1,3,256,1280]{3,2,1,0:T(8,128)(2,1)} %param.5) | data formatting | bytes 3932160 | tf_op args[0]
  12.0 0.0 copy-start.2
  12.0 7.4 %all-to-all-start = ((bf16[1,3,256,1280]{3,1,0,2:T(4,128)(2,1)}), bf16[1,3,256,1280]{3,1,0,2:T(4,128)(2,1)S(1)}, u32[]{:S(2)}, u32[]{:S(2)}) async-start(bf16[1,3,256,1280]{3,1,0,2:T(4,128)(2,1)} %copy.35), calls=%async_computation | async-start | bytes 5242880 | tf_op jit(solution)/shard_map/all_to_all | solution.py:43
  19.4 0.0 all-gather.5.cloned.1.call-start
  19.5 0.7 all-gather.5.cloned.1.call-update
  20.2 0.0 copy-done.2
  20.2 0.1 broadcast_compare_fusion
  20.3 58.6 %all-to-all-done = bf16[1,3,256,1280]{3,1,0,2:T(4,128)(2,1)S(1)} async-done(((bf16[1,3,256,1280]{3,1,0,2:T(4,128)(2,1)}), bf16[1,3,256,1280]{3,1,0,2:T(4,128)(2,1)S(1)}, u32[]{:S(2)}, u32[]{:S(2)}) %all-to-all-start) | async-done | bytes 1966112 | tf_op jit(solution)/shard_map/all_to_all | solution.py:43
  78.9 2.3 %convert_bitcast_fusion = (f32[1,8,3,32,1280]{4,3,1,2,0:T(8,128)}, bf16[1,3,256,1280]{3,2,1,0:T(8,128)(2,1)S(1)}) fusion(bf16[1,3,256,1280]{3,1,0,2:T(4,128)(2,1)S(1)} %all-to-all-done), kind=kLoop, calls=%fused_computation.1 | loop fusion | flops 983040 | bytes 7864320 | tf_op jit(solution)/shard_map/convert_element_type | solution.py:14
  81.2 0.3 fusion.5
  81.6 0.7 multiply_reduce_fusion
  82.3 0.1 rsqrt.12
  82.4 0.1 div.17
  82.4 0.0 copy-start.1
  82.4 2.4 %copy.37 = f32[1,8,3,32,1280]{4,3,2,1,0:T(8,128)S(1)} copy(f32[1,8,3,32,1280]{4,3,1,2,0:T(8,128)} %get-tuple-element.5) | data formatting | bytes 7864320 | tf_op jit(solution)/shard_map/convert_element_type | solution.py:14
  84.9 0.0 copy-done.1
  84.9 0.6 fusion.2
  85.4 0.0 all-gather.3.cloned.1.call-done
  85.5 8.5 %fusion.18 = (bf16[768,1920]{1,0:T(8,128)(2,1)S(1)}, f32[768,1920]{1,0:T(8,128)}) fusion(bf16[768,1280]{1,0:T(8,128)(2,1)S(1)} %fusion.2, bf16[1280,1920]{0,1:T(8,128)(2,1)} %all-gather.3.cloned.1.call-done), kind=kOutput, calls=%fused_computation.27 | convolution fusion | flops 3776348160 | bytes 15728640 | tf_op jit(solution)/shard_map/dot_general | solution.py:48
  94.0 0.2 fusion.17
  94.2 1.6 %reshape.90 = bf16[24,32,8,80]{3,2,1,0:T(8,128)(2,1)S(1)} reshape(bf16[768,640]{1,0:T(8,128)(2,1)S(1)} %get-tuple-element.8) | data formatting | bytes 1966080 | tf_op jit(solution)/shard_map/reshape | solution.py:55
  95.8 1.7 %fusion.6 = bf16[768,640]{1,0:T(8,128)(2,1)S(1)} fusion(f32[768,1920]{1,0:T(8,128)} %get-tuple-element.10), kind=kLoop, calls=%fused_computation.13 | loop fusion | flops 983040 | bytes 2949120 | tf_op jit(solution)/shard_map/convert_element_type | solution.py:21
  97.5 2.5 %reshape.89 = bf16[24,32,8,80]{3,2,1,0:T(8,128)(2,1)} reshape(bf16[768,640]{1,0:T(8,128)(2,1)S(1)} %fusion.6) | data formatting | bytes 1966080 | tf_op jit(solution)/shard_map/reshape | solution.py:55
  100.0 5.7 %fusion.4 = (f32[32,8,24]{2,1,0:T(8,128)S(1)}, f32[32,8,24,24]{2,3,1,0:T(8,128)}) fusion(pred[24,24]{0,1:T(8,128)(4,1)S(1)} %broadcast_compare_fusion, bf16[24,32,8,80]{3,2,1,0:T(8,128)(2,1)S(1)} %reshape.90, bf16[24,32,8,80]{3,2,1,0:T(8,128)(2,1)} %reshape.89), kind=kOutput, calls=%fused_computation.10 | convolution fusion | flops 23881728 | bytes 2581056 | tf_op jit(solution)/shard_map/flhe,glhe->lhfg/dot_general | solution.py:28
  105.7 1.6 %reshape.88 = bf16[24,32,8,80]{3,2,1,0:T(8,128)(2,1)S(1)} reshape(bf16[768,640]{1,0:T(8,128)(2,1)S(1)} %get-tuple-element.7) | data formatting | bytes 1966080 | tf_op jit(solution)/shard_map/reshape | solution.py:55
  107.3 3.4 %fusion.13 = bf16[24,32,8,80]{3,0,2,1:T(8,128)(2,1)S(1)} fusion(f32[32,8,24,24]{2,3,1,0:T(8,128)} %get-tuple-element.12, f32[32,8,24]{2,1,0:T(8,128)S(1)} %get-tuple-element.11, pred[24,24]{0,1:T(8,128)(4,1)S(1)} %broadcast_compare_fusion, bf16[24,32,8,80]{3,2,1,0:T(8,128)(2,1)S(1)} %reshape.88), kind=kOutput, calls=%fused_computation.21 | convolution fusion | flops 24526848 | bytes 2581056 | tf_op jit(solution)/shard_map/lhfg,glhe->flhe/dot_general | solution.py:32
  110.7 0.3 copy.44
  111.1 1.2 reshape.91
  112.3 0.0 copy-start
  112.3 28.2 %all_to_all.24 = bf16[1,24,32,640]{3,2,0,1:T(8,128)(2,1)S(1)} all-to-all(bf16[1,24,32,640]{3,2,0,1:T(8,128)(2,1)S(1)} %bitcast.36), channel_id=1, replica_groups=mesh['dp'=4,'seq'=8] {'seq'}, dimensions={1} | all-to-all | bytes 1966080 | tf_op jit(solution)/shard_map/all_to_all | solution.py:57
  140.5 0.1 copy.46
  140.6 0.0 all-gather.5.cloned.1.call-done
  140.6 0.0 copy-done
  140.6 4.4 %fusion.3 = bf16[768,1280]{1,0:T(8,128)(2,1)} fusion(bf16[768,640]{1,0:T(8,128)(2,1)S(1)} %bitcast.39, bf16[640,1280]{0,1:T(8,128)(2,1)} %all-gather.5.cloned.1.call-done, bf16[768,1280]{1,0:T(8,128)(2,1)S(1)} %bitcast.38), kind=kOutput, calls=%fused_computation.7 | convolution fusion | flops 1261240320 | bytes 6553600 | tf_op jit(solution)/shard_map/dot_general | solution.py:64
  (4 shorter events, 0.0 us)
Async XLA Ops:
  6.5 78.9 %all-gather.3.cloned.1.call-start = ((), (), s32[]{:S(2)}) async-start(), calls=%async_computation.2 | async-start | bytes 6144000 | tf_op jit(solution)/shard_map/all_gather | solution.py:51
  12.0 8.2 %copy-start.2 = (s32[1,24]{1,0:T(1,128)S(1)}, s32[1,24]{1,0:T(1,128)}, u32[]{:S(2)}) copy-start(s32[1,24]{1,0:T(1,128)} %param.6) | copy-start | bytes 292
  12.0 66.9 %all-to-all-start = ((bf16[1,3,256,1280]{3,1,0,2:T(4,128)(2,1)}), bf16[1,3,256,1280]{3,1,0,2:T(4,128)(2,1)S(1)}, u32[]{:S(2)}, u32[]{:S(2)}) async-start(bf16[1,3,256,1280]{3,1,0,2:T(4,128)(2,1)} %copy.35), calls=%async_computation | async-start | bytes 5242880 | tf_op jit(solution)/shard_map/all_to_all | solution.py:43
  19.4 121.2 %all-gather.5.cloned.1.call-start = ((), (), s32[]{:S(2)}) async-start(), calls=%async_computation.3 | async-start | bytes 2048000 | tf_op jit(solution)/shard_map/all_gather | solution.py:66
  82.4 2.4 %copy-start.1 = (f32[1280]{0:T(1024)S(1)}, f32[1280]{0:T(1024)}, u32[]{:S(2)}) copy-start(f32[1280]{0:T(1024)} %param.7) | copy-start | bytes 15364
  112.3 28.3 %copy-start = (bf16[1,3,256,1280]{3,2,1,0:T(8,128)(2,1)S(1)}, bf16[1,3,256,1280]{3,2,1,0:T(8,128)(2,1)}, u32[]{:S(2)}) copy-start(bf16[1,3,256,1280]{3,2,1,0:T(8,128)(2,1)} %param.5) | copy-start | bytes 5898244
Sparse Core Ops, SparseCore 0:
  8.9 41.2 all-gather.2
  51.8 19.9 all-gather.4
where the time goes:
time: 152 us
  waiting for transfers between devices  60.1 us (40%)
  blocking collectives  28.2 us (19%)
  matrix products  22 us (14%)
  local copies, waits for them, and re-layouts  14.9 us (10%)
  between operations  13.6 us (9%)
  starting transfers between devices  7.45 us (5%)
  other arithmetic  5.69 us (4%)
    all_to_all x1, waiting for transfers between devices, shards(): lax.all_to_all(tokens, 'seq', split_axis=2, concat_axis=1, tiled=True)  58.6 us
    all_to_all x1, blocking collectives, shards(): lax.all_to_all(mixed.reshape(1, frames, places, HD), 'seq', split_axis=1,...  28.2 us
    dot_general x1, matrix products, column_block(): return jnp.dot(normed, piece, preferred_element_type=jnp.float32)  8.52 us
    all_to_all x1, starting transfers between devices, shards(): lax.all_to_all(tokens, 'seq', split_axis=2, concat_axis=1, tiled=True)  7.41 us
    dot_general x1, matrix products, attend(): jnp.einsum('flhe,glhe->lhfg', queries, keys, preferred_element_type=jnp.f...  5.69 us
    unnamed x7, local copies, waits for them, and re-layouts  4.77 us
    dot_general x1, matrix products, column_block(): return jnp.dot(rows_in, piece, preferred_element_type=jnp.float32)  4.43 us
    dot_general x1, matrix products, attend(): jnp.einsum('lhfg,glhe->flhe', attn_probs, values, preferred_element_type=...  3.4 us
  transfers between devices with their start and end apart: 3, of which 1 were waited for; matrix products, arithmetic and copies ran while one was open for 25% of the time, Pallas kernels for 0%

commit v1 on v0

--- a/solution.py
+++ b/solution.py
@@ -8,6 +8,28 @@
 HEADS = 8
 HD = 640
 norm_eps = 1e-05
+
+
+def split_up(x, dim, size):
+    before, after = (x.shape[:dim], x.shape[dim + 1 :])
+    return jnp.moveaxis(x.reshape(*before, size, -1, *after), dim, 0)
+
+
+def in_order(blocks, dim):
+    lengths = list(blocks.shape[1:])
+    lengths[dim] *= blocks.shape[0]
+    return jnp.moveaxis(blocks, 0, dim).reshape(lengths)
+
+
+def rotated_exchange(x, axis, split_dim, concat_dim):
+    peers, place = (lax.axis_size(axis), lax.axis_index(axis))
+    blocks = split_up(x, split_dim, peers)
+    outs = [blocks[place]]
+    for step in range(1, peers):
+        sent = blocks[(place + step) % peers]
+        outs.append(lax.ppermute(sent, axis, [(i, (i + step) % peers) for i in range(peers)]))
+    blocks = jnp.stack(outs)[(place - jnp.arange(peers)) % peers]
+    return in_order(blocks, concat_dim)
 
 
 def layer_norm(block, ln_gain):
@@ -54,9 +76,7 @@
     mixed = attend(
         queries.reshape(head_shape), keys.reshape(head_shape), values.reshape(head_shape), clip_row
     )
-    mixed = lax.all_to_all(
-        mixed.reshape(1, frames, places, HD), "seq", split_axis=1, concat_axis=2, tiled=True
-    )
+    mixed = rotated_exchange(mixed.reshape(1, frames, places, HD), "seq", 1, 2)
     row_count = local_frames * patches
     rows_in = mixed.reshape(row_count, HD)
 

time: 152 us -> 149 us (0.980)
  the two profiles are of different devices: /device:TPU:0 before, /device:TPU:15 now
where the time goes in v1:
time: 149 us
  waiting for transfers between devices  75.7 us (51%)
  matrix products  19.6 us (13%)
  local copies, waits for them, and re-layouts  18.7 us (13%)
  starting transfers between devices  15.1 us (10%)
  between operations  13.7 us (9%)
  other arithmetic  5.95 us (4%)
    all_to_all x1, waiting for transfers between devices, shards(): lax.all_to_all(tokens, 'seq', split_axis=2, concat_axis=1, tiled=True)  56 us
    ppermute x7, waiting for transfers between devices, rotated_exchange(): lax.ppermute(sent, axis, [(i, (i + step) % peers) for i in range(peers)])  18.2 us
    ppermute x7, starting transfers between devices, rotated_exchange(): lax.ppermute(sent, axis, [(i, (i + step) % peers) for i in range(peers)])  9.33 us
    dot_general x1, matrix products, column_block(): return jnp.dot(normed, piece, preferred_element_type=jnp.float32)  8.5 us
    unnamed x13, local copies, waits for them, and re-layouts  5.8 us
    all_to_all x1, starting transfers between devices, shards(): lax.all_to_all(tokens, 'seq', split_axis=2, concat_axis=1, tiled=True)  5.79 us
    dot_general x1, matrix products, column_block(): return jnp.dot(rows_in, piece, preferred_element_type=jnp.float32)  5.04 us
    dot_general x1, matrix products, attend(): jnp.einsum('flhe,glhe->lhfg', queries, keys, preferred_element_type=jnp.f...  4.53 us
  transfers between devices with their start and end apart: 10, of which 5 were waited for; matrix products, arithmetic and copies ran while one was open for 26% of the time, Pallas kernels for 0%

profile of v1, /device:TPU:15, one launch (start us, length us, event | category | flops | bytes accessed | tf_op | source)
XLA Modules:
  0.0 148.7 jit_solution(8083725729783395908)
XLA Ops:
  6.5 0.0 all-gather.3.cloned.1.call-start
  6.5 0.7 all-gather.3.cloned.1.call-update
  7.3 4.7 %copy.24 = bf16[1,3,256,1280]{3,1,0,2:T(4,128)(2,1)} copy(bf16[1,3,256,1280]{3,2,1,0:T(8,128)(2,1)} %param.5) | data formatting | bytes 3932160 | tf_op args[0]
  12.0 0.0 copy-start.2
  12.0 5.8 %all-to-all-start = ((bf16[1,3,256,1280]{3,1,0,2:T(4,128)(2,1)}), bf16[1,3,256,1280]{3,1,0,2:T(4,128)(2,1)S(1)}, u32[]{:S(2)}, u32[]{:S(2)}) async-start(bf16[1,3,256,1280]{3,1,0,2:T(4,128)(2,1)} %copy.24), calls=%async_computation | async-start | bytes 5242880 | tf_op jit(solution)/shard_map/all_to_all | solution.py:65
  17.8 0.0 all-gather.5.cloned.1.call-start
  17.8 0.7 all-gather.5.cloned.1.call-update
  18.6 0.0 copy-done.2
  18.6 0.1 broadcast_compare_fusion
  18.7 56.0 %all-to-all-done = bf16[1,3,256,1280]{3,1,0,2:T(4,128)(2,1)S(1)} async-done(((bf16[1,3,256,1280]{3,1,0,2:T(4,128)(2,1)}), bf16[1,3,256,1280]{3,1,0,2:T(4,128)(2,1)S(1)}, u32[]{:S(2)}, u32[]{:S(2)}) %all-to-all-start) | async-done | bytes 1966112 | tf_op jit(solution)/shard_map/all_to_all | solution.py:65
  74.7 0.5 convert_bitcast_fusion
  75.2 0.3 fusion.5
  75.6 0.7 multiply_reduce_fusion
  76.2 0.0 copy-start.1
  76.2 2.1 %copy.26 = f32[1,8,3,32,1280]{4,3,2,1,0:T(8,128)} copy(f32[1,8,3,32,1280]{4,3,1,2,0:T(8,128)S(1)} %get-tuple-element.5) | data formatting | bytes 7864320 | tf_op jit(solution)/shard_map/convert_element_type | solution.py:36
  78.4 0.1 rsqrt.12
  78.5 0.1 div.17
  78.6 0.0 copy-done.1
  78.6 2.7 %fusion.2 = bf16[768,1280]{1,0:T(8,128)(2,1)S(1)} fusion(f32[1,8,3,32,1280]{4,3,2,1,0:T(8,128)} %copy.26, f32[1280]{0:T(1024)S(1)} %copy-done.1, f32[768]{0:T(1024)S(1)} %rsqrt.12, f32[768]{0:T(1024)S(1)} %div.17), kind=kLoop, calls=%fused_computation.6 | loop fusion | flops 3932160 | bytes 5909504 | tf_op jit(solution)/shard_map/convert_element_type | solution.py:39
  81.2 0.0 all-gather.3.cloned.1.call-done
  81.3 8.5 %fusion.20 = (bf16[768,1920]{1,0:T(8,128)(2,1)S(1)}, f32[768,1920]{1,0:T(8,128)}) fusion(bf16[768,1280]{1,0:T(8,128)(2,1)S(1)} %fusion.2, bf16[1280,1920]{0,1:T(8,128)(2,1)} %all-gather.3.cloned.1.call-done), kind=kOutput, calls=%fused_computation.50 | convolution fusion | flops 3776348160 | bytes 15728640 | tf_op jit(solution)/shard_map/dot_general | solution.py:70
  89.8 0.2 fusion.19
  89.9 2.5 %reshape.132 = bf16[24,32,8,80]{3,2,1,0:T(8,128)(2,1)} reshape(bf16[768,640]{1,0:T(8,128)(2,1)S(1)} %get-tuple-element.8) | data formatting | bytes 1966080 | tf_op jit(solution)/shard_map/reshape | solution.py:77
  92.4 1.7 %fusion.6 = bf16[768,640]{1,0:T(8,128)(2,1)S(1)} fusion(f32[768,1920]{1,0:T(8,128)} %get-tuple-element.18), kind=kLoop, calls=%fused_computation.14 | loop fusion | flops 983040 | bytes 2949120 | tf_op jit(solution)/shard_map/convert_element_type | solution.py:43
  94.2 2.5 %reshape.131 = bf16[24,32,8,80]{3,2,1,0:T(8,128)(2,1)} reshape(bf16[768,640]{1,0:T(8,128)(2,1)S(1)} %fusion.6) | data formatting | bytes 1966080 | tf_op jit(solution)/shard_map/reshape | solution.py:77
  96.7 1.6 %reshape.130 = bf16[24,32,8,80]{3,2,1,0:T(8,128)(2,1)S(1)} reshape(bf16[768,640]{1,0:T(8,128)(2,1)S(1)} %get-tuple-element.7) | data formatting | bytes 1966080 | tf_op jit(solution)/shard_map/reshape | solution.py:77
  98.3 4.5 %fusion.4 = (f32[32,8,24]{2,1,0:T(8,128)S(1)}, f32[32,8,24,24]{2,3,1,0:T(8,128)S(1)}) fusion(pred[24,24]{0,1:T(8,128)(4,1)S(1)} %broadcast_compare_fusion, bf16[24,32,8,80]{3,2,1,0:T(8,128)(2,1)} %reshape.132, bf16[24,32,8,80]{3,2,1,0:T(8,128)(2,1)} %reshape.131), kind=kOutput, calls=%fused_computation.11 | convolution fusion | flops 23881728 | bytes 2581056 | tf_op jit(solution)/shard_map/flhe,glhe->lhfg/dot_general | solution.py:50
  102.8 1.5 %fusion.13 = bf16[24,32,8,80]{3,0,2,1:T(8,128)(2,1)S(1)} fusion(f32[32,8,24,24]{2,3,1,0:T(8,128)S(1)} %get-tuple-element.20, f32[32,8,24]{2,1,0:T(8,128)S(1)} %get-tuple-element.19, pred[24,24]{0,1:T(8,128)(4,1)S(1)} %broadcast_compare_fusion, bf16[24,32,8,80]{3,2,1,0:T(8,128)(2,1)S(1)} %reshape.130), kind=kOutput, calls=%fused_computation.22 | convolution fusion | flops 24526848 | bytes 2581056 | tf_op jit(solution)/shard_map/lhfg,glhe->flhe/dot_general | solution.py:54
  104.4 0.3 copy.33
  104.7 1.2 transpose_reshape_reshape.3
  105.9 0.1 dynamic-slice_bitcast_fusion
  106.1 0.1 collective-permute-start
  106.2 4.1 %collective-permute-start.1 = (bf16[1,3,32,640]{3,2,1,0:T(8,128)(2,1)S(1)}, bf16[1,3,32,640]{3,2,1,0:T(8,128)(2,1)S(1)}, u32[]{:S(2)}, u32[]{:S(2)}) collective-permute-start(bf16[1,3,32,640]{3,2,1,0:T(8,128)(2,1)S(1)} %get-tuple-element.14), channel_id=1, source_target_pairs={{0,2},{1,3},{2,4},{3,5},{4,6},{5,7},{6,0},{7,1},{8,10},{9,11},{10,... | collective-permute-start | bytes 368648 | tf_op jit(solution)/shard_map/ppermute | solution.py:30
  110.3 1.3 collective-permute-start.2
  111.6 0.0 collective-permute-start.3
  111.6 1.4 collective-permute-start.4
  112.9 0.0 collective-permute-done
  112.9 1.9 %collective-permute-start.5 = (bf16[1,3,32,640]{3,2,1,0:T(8,128)(2,1)S(1)}, bf16[1,3,32,640]{3,2,1,0:T(8,128)(2,1)S(1)}, u32[]{:S(2)}, u32[]{:S(2)}) collective-permute-start(bf16[1,3,32,640]{3,2,1,0:T(8,128)(2,1)S(1)} %get-tuple-element.10), channel_id=1, source_target_pairs={{0,6},{1,7},{2,0},{3,1},{4,2},{5,3},{6,4},{7,5},{8,14},{9,15},{10,... | collective-permute-start | bytes 368648 | tf_op jit(solution)/shard_map/ppermute | solution.py:30
  114.8 0.0 collective-permute-done.1
  114.8 0.6 collective-permute-start.6
  115.5 9.9 %collective-permute-done.2 = bf16[1,3,32,640]{3,2,1,0:T(8,128)(2,1)S(1)} collective-permute-done((bf16[1,3,32,640]{3,2,1,0:T(8,128)(2,1)S(1)}, bf16[1,3,32,640]{3,2,1,0:T(8,128)(2,1)S(1)}, u32[]{:S(2)}, u32[]{:S(2)}) %collective-permute-start.2) | collective-permute-done | bytes 122912 | tf_op jit(solution)/shard_map/ppermute | solution.py:30
  125.4 2.6 %collective-permute-done.3 = bf16[1,3,32,640]{3,2,1,0:T(8,128)(2,1)S(1)} collective-permute-done((bf16[1,3,32,640]{3,2,1,0:T(8,128)(2,1)S(1)}, bf16[1,3,32,640]{3,2,1,0:T(8,128)(2,1)S(1)}, u32[]{:S(2)}, u32[]{:S(2)}) %collective-permute-start.3) | collective-permute-done | bytes 122912 | tf_op jit(solution)/shard_map/ppermute | solution.py:30
  128.0 0.0 collective-permute-done.4
  128.1 4.1 %collective-permute-done.5 = bf16[1,3,32,640]{3,2,1,0:T(8,128)(2,1)S(1)} collective-permute-done((bf16[1,3,32,640]{3,2,1,0:T(8,128)(2,1)S(1)}, bf16[1,3,32,640]{3,2,1,0:T(8,128)(2,1)S(1)}, u32[]{:S(2)}, u32[]{:S(2)}) %collective-permute-start.5) | collective-permute-done | bytes 122912 | tf_op jit(solution)/shard_map/ppermute | solution.py:30
  132.2 1.6 %collective-permute-done.6 = bf16[1,3,32,640]{3,2,1,0:T(8,128)(2,1)S(1)} collective-permute-done((bf16[1,3,32,640]{3,2,1,0:T(8,128)(2,1)S(1)}, bf16[1,3,32,640]{3,2,1,0:T(8,128)(2,1)S(1)}, u32[]{:S(2)}, u32[]{:S(2)}) %collective-permute-start.6) | collective-permute-done | bytes 122912 | tf_op jit(solution)/shard_map/ppermute | solution.py:30
  133.8 0.0 copy-start
  133.8 0.9 copy-done
  134.8 1.9 %gather_fusion = bf16[8,3,32,640]{3,2,1,0:T(8,128)(2,1)S(1)} fusion(bf16[8,3,32,640]{3,2,1,0:T(8,128)(2,1)} %bitcast.68, s32[1024]{0:T(1024)S(1)} %pad_clamp_fusion), kind=kCustom, calls=%fused_computation | custom fusion | bytes 1966112 | tf_op jit(solution)/shard_map/gather | solution.py:31
  136.7 0.1 copy.34
  136.8 0.0 all-gather.5.cloned.1.call-done
  136.9 5.0 %fusion.3 = bf16[768,1280]{1,0:T(8,128)(2,1)} fusion(bf16[768,640]{1,0:T(8,128)(2,1)S(1)} %bitcast.69, bf16[640,1280]{0,1:T(8,128)(2,1)} %all-gather.5.cloned.1.call-done, bf16[768,1280]{1,0:T(8,128)(2,1)} %bitcast.67), kind=kOutput, calls=%fused_computation.8 | convolution fusion | flops 1261240320 | bytes 6553600 | tf_op jit(solution)/shard_map/dot_general | solution.py:84
  (13 shorter events, 0.2 us)
Async XLA Ops:
  6.5 74.7 %all-gather.3.cloned.1.call-start = ((), (), s32[]{:S(2)}) async-start(), calls=%async_computation.1 | async-start | bytes 6144000 | tf_op jit(solution)/shard_map/all_gather | solution.py:73
  12.0 6.6 %copy-start.2 = (s32[1,24]{1,0:T(1,128)S(1)}, s32[1,24]{1,0:T(1,128)}, u32[]{:S(2)}) copy-start(s32[1,24]{1,0:T(1,128)} %param.6) | copy-start | bytes 292
  12.0 62.7 %all-to-all-start = ((bf16[1,3,256,1280]{3,1,0,2:T(4,128)(2,1)}), bf16[1,3,256,1280]{3,1,0,2:T(4,128)(2,1)S(1)}, u32[]{:S(2)}, u32[]{:S(2)}) async-start(bf16[1,3,256,1280]{3,1,0,2:T(4,128)(2,1)} %copy.24), calls=%async_computation | async-start | bytes 5242880 | tf_op jit(solution)/shard_map/all_to_all | solution.py:65
  17.8 119.1 %all-gather.5.cloned.1.call-start = ((), (), s32[]{:S(2)}) async-start(), calls=%async_computation.2 | async-start | bytes 2048000 | tf_op jit(solution)/shard_map/all_gather | solution.py:86
  76.2 2.3 %copy-start.1 = (f32[1280]{0:T(1024)S(1)}, f32[1280]{0:T(1024)}, u32[]{:S(2)}) copy-start(f32[1280]{0:T(1024)} %param.7) | copy-start | bytes 15364
  106.1 6.9 %collective-permute-start = (bf16[1,3,32,640]{3,2,1,0:T(8,128)(2,1)S(1)}, bf16[1,3,32,640]{3,2,1,0:T(8,128)(2,1)S(1)}, u32[]{:S(2)}, u32[]{:S(2)}) collective-permute-start(bf16[1,3,32,640]{3,2,1,0:T(8,128)(2,1)S(1)} %get-tuple-element.15), channel_id=1, source_target_pairs={{0,1},{1,2},{2,3},{3,4},{4,5},{5,6},{6,7},{7,0},{8,9},{9,10},{10,1... | collective-permute-start | bytes 368648 | tf_op jit(solution)/shard_map/ppermute | solution.py:30
  106.2 8.7 %collective-permute-start.1 = (bf16[1,3,32,640]{3,2,1,0:T(8,128)(2,1)S(1)}, bf16[1,3,32,640]{3,2,1,0:T(8,128)(2,1)S(1)}, u32[]{:S(2)}, u32[]{:S(2)}) collective-permute-start(bf16[1,3,32,640]{3,2,1,0:T(8,128)(2,1)S(1)} %get-tuple-element.14), channel_id=1, source_target_pairs={{0,2},{1,3},{2,4},{3,5},{4,6},{5,7},{6,0},{7,1},{8,10},{9,11},{10,... | collective-permute-start | bytes 368648 | tf_op jit(solution)/shard_map/ppermute | solution.py:30
  110.3 15.1 %collective-permute-start.2 = (bf16[1,3,32,640]{3,2,1,0:T(8,128)(2,1)S(1)}, bf16[1,3,32,640]{3,2,1,0:T(8,128)(2,1)S(1)}, u32[]{:S(2)}, u32[]{:S(2)}) collective-permute-start(bf16[1,3,32,640]{3,2,1,0:T(8,128)(2,1)S(1)} %get-tuple-element.13), channel_id=1, source_target_pairs={{0,3},{1,4},{2,5},{3,6},{4,7},{5,0},{6,1},{7,2},{8,11},{9,12},{10,... | collective-permute-start | bytes 368648 | tf_op jit(solution)/shard_map/ppermute | solution.py:30
  111.6 16.5 %collective-permute-start.3 = (bf16[1,3,32,640]{3,2,1,0:T(8,128)(2,1)S(1)}, bf16[1,3,32,640]{3,2,1,0:T(8,128)(2,1)S(1)}, u32[]{:S(2)}, u32[]{:S(2)}) collective-permute-start(bf16[1,3,32,640]{3,2,1,0:T(8,128)(2,1)S(1)} %get-tuple-element.12), channel_id=1, source_target_pairs={{0,4},{1,5},{2,6},{3,7},{4,0},{5,1},{6,2},{7,3},{8,12},{9,13},{10,... | collective-permute-start | bytes 368648 | tf_op jit(solution)/shard_map/ppermute | solution.py:30
  111.6 16.5 %collective-permute-start.4 = (bf16[1,3,32,640]{3,2,1,0:T(8,128)(2,1)S(1)}, bf16[1,3,32,640]{3,2,1,0:T(8,128)(2,1)S(1)}, u32[]{:S(2)}, u32[]{:S(2)}) collective-permute-start(bf16[1,3,32,640]{3,2,1,0:T(8,128)(2,1)S(1)} %get-tuple-element.11), channel_id=1, source_target_pairs={{0,5},{1,6},{2,7},{3,0},{4,1},{5,2},{6,3},{7,4},{8,13},{9,14},{10,... | collective-permute-start | bytes 368648 | tf_op jit(solution)/shard_map/ppermute | solution.py:30
  112.9 19.3 %collective-permute-start.5 = (bf16[1,3,32,640]{3,2,1,0:T(8,128)(2,1)S(1)}, bf16[1,3,32,640]{3,2,1,0:T(8,128)(2,1)S(1)}, u32[]{:S(2)}, u32[]{:S(2)}) collective-permute-start(bf16[1,3,32,640]{3,2,1,0:T(8,128)(2,1)S(1)} %get-tuple-element.10), channel_id=1, source_target_pairs={{0,6},{1,7},{2,0},{3,1},{4,2},{5,3},{6,4},{7,5},{8,14},{9,15},{10,... | collective-permute-start | bytes 368648 | tf_op jit(solution)/shard_map/ppermute | solution.py:30
  114.8 19.0 %collective-permute-start.6 = (bf16[1,3,32,640]{3,2,1,0:T(8,128)(2,1)S(1)}, bf16[1,3,32,640]{3,2,1,0:T(8,128)(2,1)S(1)}, u32[]{:S(2)}, u32[]{:S(2)}) collective-permute-start(bf16[1,3,32,640]{3,2,1,0:T(8,128)(2,1)S(1)} %get-tuple-element.9), channel_id=1, source_target_pairs={{0,7},{1,0},{2,1},{3,2},{4,3},{5,4},{6,5},{7,6},{8,15},{9,8},{10,9... | collective-permute-start | bytes 368648 | tf_op jit(solution)/shard_map/ppermute | solution.py:30
  133.8 0.9 copy-start
Sparse Core Ops, SparseCore 0:
  8.9 39.1 all-gather.2
  49.6 19.9 all-gather.4
